TPU v7x, 512 devices: a whole 4x4x16 slice. The times are simulated.
512 devices in a mesh: var: 128 (over y, x, z_lo, core), samp: 4 (over z_hi).
Axes of the slice: x: 4, y: 4, z: 16 (z_hi: 4, z_lo: 4; z = z_hi * 4 + z_lo), core: 2. Of those that a mesh axis runs over, the one named last changes fastest.
Arguments:
- dosages: int32 [1024, 131072], P('samp', 'var'), may hold values from 0 to 3, as said below
- weights: bfloat16 [131072, 2560], P(('var', 'samp')), may hold values from -0.0625 to 0.0625
- variant_pass: int32 [131072], P('var'), may hold values 0 or 1
- ancestry: float32 [1024, 20], P('samp')
Outputs:
- standardized: float32 [2560, 1024], P('var', 'samp')
Inputs may be any that keep to these rules, and one draw needn't show every extreme that they name: 3 marks a missing call; other values are allele dosages.
All inputs are finite; a program needn't handle non-finite values. No bound on the sum of `variant_pass` on one device may be relied on, other than what follows from the above.
Results may differ from a plain program's by a relative error of at most 0.0024.
Values may be sent and summed in bfloat16 or wider, within the bound.
A program may use at most 64 MiB of HBM per device.

v0:
```python
import jax
import jax.numpy as jnp
from jax import lax
from jax.sharding import PartitionSpec as P


def cholesky_apply(gram, cross):
    factor = jnp.linalg.cholesky(gram)
    order_n = gram.shape[0]
    forward = []
    for row_idx in range(order_n):
        running = cross[:, row_idx]
        for col_idx in range(row_idx):
            running = running - factor[row_idx, col_idx] * forward[col_idx]
        forward.append(running / factor[row_idx, row_idx])
    solved = [None] * order_n
    for row_idx in reversed(range(order_n)):
        running = forward[row_idx]
        for col_idx in range(row_idx + 1, order_n):
            running = running - factor[col_idx, row_idx] * solved[col_idx]
        solved[row_idx] = running / factor[row_idx, row_idx]
    return jnp.stack(solved, axis=1)


def on_device(dosages, weights, variant_pass, ancestry):
    samples_here = dosages.shape[0]
    total_samples = samples_here * lax.axis_size("samp")
    observed = dosages < 3
    allele_total, observed_count = lax.psum(
        (
            jnp.sum(jnp.where(observed, dosages, 0).astype(jnp.float32), axis=0),
            jnp.sum(observed.astype(jnp.float32), axis=0),
        ),
        "samp",
    )
    impute = ((allele_total + 1.0) / (observed_count + 1.0)).astype(jnp.bfloat16)
    genotypes = jnp.where(observed, dosages.astype(jnp.bfloat16), impute[None, :])
    genotypes = genotypes * variant_pass.astype(jnp.bfloat16)[None, :]
    full_weights = lax.all_gather(weights, "samp", axis=0, tiled=True)
    every_score = lax.dot_general(
        full_weights, genotypes, (((0,), (1,)), ((), ())), preferred_element_type=jnp.float32
    )
    raw_scores = lax.psum_scatter(every_score, "var", scatter_dimension=0, tiled=True)
    design = jnp.concatenate([jnp.ones((samples_here, 1), jnp.float32), ancestry], axis=1)
    local_gram = jnp.dot(design.T, design, precision=lax.Precision.HIGHEST)
    local_cross = jnp.dot(raw_scores, design, precision=lax.Precision.HIGHEST)
    gram = lax.psum(local_gram, "samp")
    cross = lax.psum(local_cross, "samp")
    coeffs = cholesky_apply(gram, cross)
    residual = raw_scores - jnp.dot(coeffs, design.T, precision=lax.Precision.HIGHEST)
    squared = lax.psum(jnp.sum(residual * residual, axis=1), "samp")
    spread = squared / (total_samples - 1)
    return residual / jnp.sqrt(spread + 1e-06)[:, None]


def solution(mesh):
    in_specs = (P("samp", "var"), P(("var", "samp"), None), P("var"), P("samp", None))
    out_specs = P("var", "samp")
    return jax.shard_map(
        on_device, mesh=mesh, in_specs=in_specs, out_specs=out_specs, check_vma=False
    )
```

profile of v0, /device:TPU:128, one launch (start us, length us, event | category | flops | bytes accessed | tf_op | source)
XLA Modules:
  0.0 2035.9 jit_solution(5791186550489858896)
XLA Ops:
  6.5 0.0 all-gather.2.cloned.1.call-start
  6.5 0.7 all-gather.2.cloned.1.call-update
  7.3 0.0 all-reduce.6.cloned.1.call-start
  7.3 0.7 convert_element_type.19
  8.0 1.4 convert_reduce_fusion.1
  9.4 17.7 all-reduce.3
  27.2 180.4 %all-gather.2.cloned.1.call-done = bf16[1024,2560]{1,0:T(8,128)(2,1)} async-done(((bf16[256,2560]{1,0:T(8,128)(2,1)}), bf16[1024,2560]{1,0:T(8,128)(2,1)}) %all-gather.2.cloned.1.call-update) | async-done | bytes 5242896 | tf_op jit(solution)/shard_map/all_gather | solution.py:39
  207.6 6.2 convolution_bitcast_fusion
  213.8 0.0 copy-start
  213.8 0.0 all-reduce.6.cloned.1.call-update
  213.8 1.3 dynamic-slice
  215.7 0.0 copy-done
  215.7 0.1 fusion.6
  215.9 1290.2 %all-reduce.6.cloned.1.call-done = f32[2560,256]{0,1:T(8,128)} async-done(((f32[2560,256]{0,1:T(8,128)}), f32[2560,256]{0,1:T(8,128)}) %all-reduce.6.cloned.1.call-update) | async-done | bytes 2621456
  1506.1 1.0 constant_dynamic-slice_fusion
  1507.1 0.2 fusion.8
  1507.3 22.7 %all-reduce.2 = (f32[20,21]{0,1:T(8,128)S(1)}, f32[21,21]{0,1:T(8,128)S(1)}) all-reduce(f32[20,21]{0,1:T(8,128)S(1)} %fusion.8, f32[21,21]{0,1:T(8,128)S(1)} %fusion.6), channel_id=1, replica_groups=mesh['var'=128,'samp'=4] {'samp'}, use_global_device_ids=true, to_apply=%region_5.6 | all-reduce | flops 861 | bytes 6888 | tf_op jit(solution)/shard_map/psum | solution.py:48
  1530.0 0.1 copy.42
  1530.1 1.9 cholesky.18
  1532.1 0.6 compare_reduce_fusion
  1532.7 0.6 select_select_fusion
  1533.4 0.7 fusion.84
  1534.1 0.7 fusion.83
  1534.8 0.7 fusion.82
  1535.5 0.7 fusion.90
  1536.2 0.7 fusion.91
  1537.0 0.7 fusion.89
  1537.7 0.7 fusion.81
  1538.4 0.7 fusion.86
  1539.2 0.7 fusion.85
  1539.9 0.7 fusion.87
  1540.6 0.7 fusion.88
  1541.3 0.7 fusion.92
  1542.0 0.7 fusion.80
  1542.7 0.1 copy.43
  1544.0 131.0 %subtract_divide_fusion.13 = (f32[20,1]{0,1:T(1,128)S(1)}, f32[20,1]{0,1:T(1,128)S(1)}, f32[20,1]{0,1:T(1,128)S(1)}, f32[20,1]{0,1:T(1,128)S(1)}, f32[20,1]{0,1:...) fusion(f32[20,21]{0,1:T(8,128)S(1)} %get-tuple-element.7, ...), kind=kLoop, calls=%fused_computation.141 | loop fusion | flops 8000 | bytes 4040 | tf_op jit(solution)/shard_map/div | solution.py:15
  1675.0 130.2 %subtract_divide_fusion.52 = (f32[20]{0:T(128)S(1)}, f32[20]{0:T(128)S(1)}, f32[20]{0:T(128)S(1)}, f32[20]{0:T(128)S(1)}, f32[20]{0:T(128)S(1)}, /*index=5*/f32[...) fusion(f32[20,1]{0,1:T(1,128)S(1)} %get-tuple-element.43, ...), kind=kLoop, calls=%fused_computation.181 | loop fusion | flops 7980 | bytes 3956 | tf_op jit(solution)/shard_map/div | solution.py:15
  1805.3 61.1 %subtract_divide_fusion.39 = (f32[20]{0:T(128)S(1)}, f32[20]{0:T(128)S(1)}, f32[20]{0:T(128)S(1)}, f32[20]{0:T(128)S(1)}, f32[20]{0:T(128)S(1)}, /*index=5*/f32[...) fusion(f32[20]{0:T(128)S(1)} %get-tuple-element.76, ...), kind=kLoop, calls=%fused_computation.168 | loop fusion | flops 4180 | bytes 3116 | tf_op jit(solution)/shard_map/div | solution.py:21
  1866.4 87.1 %divide_bitcast_fusion = (f32[20,1]{0,1:T(1,128)S(1)}, f32[20]{0:T(128)S(1)}, f32[20]{0:T(128)S(1)}, f32[20]{0:T(128)S(1)}, f32[20]{0:T(128)S(1)}, /*index=5*/f32[20]{0:T(128)S(1)}, f32[20]{0:T(128)S(1)}, f32[20]{0:T(128)S(1)}) fusion(f32[20]{0:T(128)S(1)} %get-tuple-element.64, f32[20]{0:T(128)S(1)} %get-tuple-element.63, f32[20]{0:T(128)S(1)} %get-tuple-element.62, ...), kind=kLoop, calls=%fused_computation.160 | loop fusion | flops 5440 | bytes 2880 | tf_op jit(solution)/shard_map/stack | solution.py:22
  1953.5 61.1 %subtract_divide_fusion = (f32[20,1]{0,1:T(1,128)S(1)}, f32[20,1]{0,1:T(1,128)S(1)}, f32[20,1]{0,1:T(1,128)S(1)}, f32[20,1]{0,1:T(1,128)S(1)}, f32[20,1]{0,1:T(1...) fusion(f32[20,1]{0,1:T(1,128)S(1)} %get-tuple-element.35, ...), kind=kLoop, calls=%fused_computation.128 | loop fusion | flops 4180 | bytes 3116 | tf_op jit(solution)/shard_map/div | solution.py:21
  2014.6 0.1 stack.48
  2014.7 0.3 multiply_reduce_fusion
  2015.0 13.4 psum.39
  2028.4 0.7 broadcast_divide_fusion
  (4 shorter events, 0.1 us)
Async XLA Ops:
  6.5 201.1 %all-gather.2.cloned.1.call-start = ((), (), s32[]{:S(2)}) async-start(), calls=%async_computation | async-start | bytes 6553600 | tf_op jit(solution)/shard_map/all_gather | solution.py:39
  7.3 1498.8 %all-reduce.6.cloned.1.call-start = ((), (), s32[]{:S(2)}) async-start(), calls=%async_computation.1 | async-start | bytes 5242880
  213.8 2.0 copy-start
Sparse Core Ops, SparseCore 0:
  9.5 198.1 all-gather.1
  213.9 1292.0 all-reduce.5
where the time goes:
time: 2040 us
  waiting for transfers between devices  1470 us (72%)
  other arithmetic  477 us (23%)
  blocking collectives  53.8 us (3%)
    unnamed x3, waiting for transfers between devices  1290 us
    div x2, other arithmetic, cholesky_apply(): forward.append(running / factor[row_idx, row_idx])  261 us
    all_gather x1, waiting for transfers between devices, on_device(): full_weights = lax.all_gather(weights, 'samp', axis=0, tiled=True)  180 us
    div x2, other arithmetic, cholesky_apply(): solved[row_idx] = running / factor[row_idx, row_idx]  122 us
    another operation x1, other arithmetic, cholesky_apply(): return jnp.stack(solved, axis=1)  87.1 us
  transfers between devices with their start and end apart: 2, of which 2 were waited for; matrix products, arithmetic and copies ran while one was open for 0% of the time, Pallas kernels for 0%

commit v1 on v0

--- a/solution.py
+++ b/solution.py
@@ -36,7 +36,10 @@
     impute = ((allele_total + 1.0) / (observed_count + 1.0)).astype(jnp.bfloat16)
     genotypes = jnp.where(observed, dosages.astype(jnp.bfloat16), impute[None, :])
     genotypes = genotypes * variant_pass.astype(jnp.bfloat16)[None, :]
-    full_weights = lax.all_gather(weights, "samp", axis=0, tiled=True)
+    n_dev = lax.axis_size("samp")
+    blocks = jnp.stack([weights for _ in range(n_dev)])
+    blocks = lax.all_to_all(blocks, "samp", split_axis=0, concat_axis=0)
+    full_weights = jnp.concatenate(blocks, axis=0)
     every_score = lax.dot_general(
         full_weights, genotypes, (((0,), (1,)), ((), ())), preferred_element_type=jnp.float32
     )

time: 2040 us -> 2090 us (1.025)
  blocking collectives: 53.8 us -> 269 us
  waiting for transfers between devices: 1470 us -> 1290 us
    psum x1, blocking collectives: 17.7 us -> 233 us  [on_device(): lax.psum((jnp.sum(jnp.where(observed, dosages, 0).astype(jnp.float32), ax...]
    all_gather x1 -> x0, waiting for transfers between devices: 180 us -> none  [on_device(): full_weights = lax.all_gather(weights, 'samp', axis=0, tiled=True)]
    unnamed x3 -> x2, waiting for transfers between devices: 1290 us -> 1290 us
  transfers between devices with their start and end apart: 2 -> 2, of which waited for: 2 -> 1; matrix products, arithmetic and copies ran while one was open for 0% -> 0% of each run, Pallas kernels for 0% -> 0%
where the time goes in v1:
time: 2090 us
  waiting for transfers between devices  1290 us (62%)
  other arithmetic  475 us (23%)
  blocking collectives  269 us (13%)
    unnamed x2, waiting for transfers between devices  1290 us
    div x2, other arithmetic, cholesky_apply(): forward.append(running / factor[row_idx, row_idx])  261 us
    psum x1, blocking collectives, on_device(): lax.psum((jnp.sum(jnp.where(observed, dosages, 0).astype(jnp.float32), ax...  233 us
    div x2, other arithmetic, cholesky_apply(): solved[row_idx] = running / factor[row_idx, row_idx]  123 us
    another operation x1, other arithmetic, cholesky_apply(): return jnp.stack(solved, axis=1)  87.3 us
  transfers between devices with their start and end apart: 2, of which 1 were waited for; matrix products, arithmetic and copies ran while one was open for 0% of the time, Pallas kernels for 0%

profile of v1, /device:TPU:128, one launch (start us, length us, event | category | flops | bytes accessed | tf_op | source)
XLA Modules:
  0.0 2085.9 jit_solution(15325980164403799498)
XLA Ops:
  6.5 4.1 stack.20
  10.6 0.0 copy-start.2
  10.6 0.0 copy-start
  10.6 14.0 all-to-all-start
  24.6 0.0 all-reduce.6.cloned.1.call-start
  24.6 0.0 copy-done.2
  24.6 0.0 copy-done
  24.6 0.2 convert_reduce_fusion.1
  24.8 233.1 %all-reduce.3 = (f32[1024]{0:T(1024)S(1)}, f32[1024]{0:T(1024)S(1)}) all-reduce(f32[1024]{0:T(1024)S(1)} %get-tuple-element.6, f32[1024]{0:T(1024)S(1)} %get-tuple-element.5), channel_id=1, replica_groups=mesh['var'=128,'samp'=4] {'samp'}, use_global_device_ids=true, to_apply=%region_3.4 | all-reduce | flops 2048 | bytes 16384 | tf_op jit(solution)/shard_map/psum | solution.py:29
  257.9 0.0 all-to-all-done
  257.9 0.0 copy-start.1
  257.9 5.5 convolution_bitcast_fusion
  263.5 0.0 all-reduce.6.cloned.1.call-update
  263.5 1.3 dynamic-slice
  265.4 0.0 copy-done.1
  265.4 0.1 fusion.6
  265.6 1289.7 %all-reduce.6.cloned.1.call-done = f32[2560,256]{0,1:T(8,128)} async-done(((f32[2560,256]{0,1:T(8,128)}), f32[2560,256]{0,1:T(8,128)}) %all-reduce.6.cloned.1.call-update) | async-done | bytes 2621456
  1555.3 1.0 constant_dynamic-slice_fusion
  1556.4 0.1 copy.43
  1556.5 0.2 fusion.8
  1556.6 22.8 %all-reduce.2 = (f32[20,21]{0,1:T(8,128)S(1)}, f32[21,21]{0,1:T(8,128)S(1)}) all-reduce(f32[20,21]{0,1:T(8,128)S(1)} %fusion.8, f32[21,21]{0,1:T(8,128)S(1)} %fusion.6), channel_id=1, replica_groups=mesh['var'=128,'samp'=4] {'samp'}, use_global_device_ids=true, to_apply=%region_5.6 | all-reduce | flops 861 | bytes 6888 | tf_op jit(solution)/shard_map/psum | solution.py:51
  1579.4 0.1 copy.42
  1579.5 1.9 cholesky.18
  1581.5 0.6 compare_reduce_fusion
  1582.1 0.6 select_select_fusion
  1582.8 0.7 fusion.81
  1583.5 0.7 fusion.89
  1584.2 0.7 fusion.90
  1585.0 0.7 fusion.91
  1585.7 0.7 fusion.92
  1586.3 0.7 fusion.82
  1587.1 0.7 fusion.83
  1587.8 0.7 fusion.84
  1588.5 0.7 fusion.85
  1589.2 0.7 fusion.86
  1590.0 0.7 fusion.87
  1590.7 0.7 fusion.88
  1591.4 0.7 fusion.80
  1592.1 131.1 %subtract_divide_fusion.13 = (f32[20,1]{0,1:T(1,128)S(1)}, f32[20,1]{0,1:T(1,128)S(1)}, f32[20,1]{0,1:T(1,128)S(1)}, f32[20,1]{0,1:T(1,128)S(1)}, f32[20,1]{0,1:...) fusion(f32[20,21]{0,1:T(8,128)S(1)} %get-tuple-element.7, ...), kind=kLoop, calls=%fused_computation.141 | loop fusion | flops 8000 | bytes 4040 | tf_op jit(solution)/shard_map/div | solution.py:15
  1723.2 130.3 %subtract_divide_fusion.52 = (f32[20]{0:T(128)S(1)}, f32[20]{0:T(128)S(1)}, f32[20]{0:T(128)S(1)}, f32[20]{0:T(128)S(1)}, f32[20]{0:T(128)S(1)}, /*index=5*/f32[...) fusion(f32[20,1]{0,1:T(1,128)S(1)} %get-tuple-element.43, ...), kind=kLoop, calls=%fused_computation.181 | loop fusion | flops 7980 | bytes 3956 | tf_op jit(solution)/shard_map/div | solution.py:15
  1854.9 61.3 %subtract_divide_fusion.39 = (f32[20]{0:T(128)S(1)}, f32[20]{0:T(128)S(1)}, f32[20]{0:T(128)S(1)}, f32[20]{0:T(128)S(1)}, f32[20]{0:T(128)S(1)}, /*index=5*/f32[...) fusion(f32[20]{0:T(128)S(1)} %get-tuple-element.76, ...), kind=kLoop, calls=%fused_computation.168 | loop fusion | flops 4180 | bytes 3116 | tf_op jit(solution)/shard_map/div | solution.py:21
  1916.2 87.3 %divide_bitcast_fusion = (f32[20,1]{0,1:T(1,128)S(1)}, f32[20]{0:T(128)S(1)}, f32[20]{0:T(128)S(1)}, f32[20]{0:T(128)S(1)}, f32[20]{0:T(128)S(1)}, /*index=5*/f32[20]{0:T(128)S(1)}, f32[20]{0:T(128)S(1)}, f32[20]{0:T(128)S(1)}) fusion(f32[20]{0:T(128)S(1)} %get-tuple-element.64, f32[20]{0:T(128)S(1)} %get-tuple-element.63, f32[20]{0:T(128)S(1)} %get-tuple-element.62, ...), kind=kLoop, calls=%fused_computation.160 | loop fusion | flops 5440 | bytes 2880 | tf_op jit(solution)/shard_map/stack | solution.py:22
  2003.4 61.3 %subtract_divide_fusion = (f32[20,1]{0,1:T(1,128)S(1)}, f32[20,1]{0,1:T(1,128)S(1)}, f32[20,1]{0,1:T(1,128)S(1)}, f32[20,1]{0,1:T(1,128)S(1)}, f32[20,1]{0,1:T(1...) fusion(f32[20,1]{0,1:T(1,128)S(1)} %get-tuple-element.35, ...), kind=kLoop, calls=%fused_computation.128 | loop fusion | flops 4180 | bytes 3116 | tf_op jit(solution)/shard_map/div | solution.py:21
  2064.7 0.1 stack.56
  2064.8 0.3 multiply_reduce_fusion
  2065.1 13.3 psum.39
  2078.4 0.7 broadcast_divide_fusion
  (5 shorter events, 0.1 us)
Async XLA Ops:
  10.6 14.0 copy-start.2
  10.6 14.0 copy-start
  10.6 247.3 %all-to-all-start = ((bf16[4,256,2560]{2,1,0:T(8,128)(2,1)}), bf16[4,256,2560]{2,1,0:T(8,128)(2,1)}, u32[]{:S(2)}, u32[]{:S(2)}) async-start(bf16[4,256,2560]{2,1,0:T(8,128)(2,1)} %stack.20), calls=%async_computation | async-start | bytes 10485760 | tf_op jit(solution)/shard_map/all_to_all | solution.py:41
  24.6 1530.8 %all-reduce.6.cloned.1.call-start = ((), (), s32[]{:S(2)}) async-start(), calls=%async_computation.1 | async-start | bytes 5242880
  257.9 7.5 copy-start.1
Sparse Core Ops, SparseCore 0:
  263.6 1291.6 all-reduce.5
